TPU v7x, 256 devices: a whole 4x4x8 slice. The times are simulated.
256 devices in a mesh: segment: 4 (over x), shard: 64 (over y, z, core).
Axes of the slice: x: 4, y: 4, z: 8, core: 2. Of those that a mesh axis runs over, the one named last changes fastest.
Arguments:
- tokens: bfloat16 [3, 128, 3072], P(None, 'shard'), may hold values from -6 to 6
- norm_gain: float32 [4, 3072], P('segment'), may hold values from 0.5 to 1.5
- w_gate: bfloat16 [4, 3072, 32768], P('segment', None, 'shard'), may hold values from -0.109375 to 0.109375
- w_up: bfloat16 [4, 3072, 32768], P('segment', None, 'shard'), may hold values from -0.109375 to 0.109375
- w_down: bfloat16 [4, 32768, 3072], P('segment', 'shard'), may hold values from -0.046875 to 0.046875
- block_counts: int32 [4], P('segment'), may hold values from 1 to 2
- gate_prob: float32 [4, 3, 128], P('segment', None, 'shard'), may hold values from 0.1 to 1
Outputs:
- section_outputs: bfloat16 [4, 3, 128, 3072], P('segment', None, 'shard')
All inputs are finite; a program needn't handle non-finite values.
Results may differ from a plain program's by a relative error of at most 0.009.
Values may be sent and summed in bfloat16 or wider, within the bound.
A program may use at most 64 MiB of HBM per device.

v0:
```python
import jax
import jax.numpy as jnp
from jax import lax
from jax.sharding import PartitionSpec as P

FF = 16384


def shifted(value, axis, steps):
    count = lax.axis_size(axis)
    initial, last = (max(0, -steps), min(count, count - steps))
    return lax.ppermute(value, axis, [(source, source + steps) for source in range(initial, last)])


def normalize(rows, row_gain):
    values = rows.astype(jnp.float32)
    scale = lax.rsqrt(jnp.mean(values * values, axis=-1, keepdims=True) + 1e-05)
    return (values * scale * row_gain).astype(jnp.bfloat16)


def expert_rows(normed, gate_part, up_part, down_part):
    gate_val = jnp.dot(normed, gate_part, preferred_element_type=jnp.float32)
    up_val = jnp.dot(normed, up_part, preferred_element_type=jnp.float32)
    hidden = (jax.nn.silu(gate_val) * up_val).astype(jnp.bfloat16)
    return jnp.dot(hidden, down_part, preferred_element_type=jnp.float32)


def shards(tokens, norm_gain, w_gate, w_up, w_down, block_counts, gate_prob):
    segment_index = lax.axis_index("segment")
    segment_count = lax.axis_size("segment")
    shard_count = lax.axis_size("shard")
    hidden_count = w_gate.shape[2]
    own_expert = lax.axis_index("shard") // (FF // hidden_count)
    zero_blocks = block_counts[0]
    row_gain = norm_gain[0]
    gate_part = w_gate[0]
    up_part = w_up[0]
    down_part = w_down[0]
    probs = gate_prob[0]
    block_total = tokens.shape[0]
    local_rows = tokens.shape[1]
    width = tokens.shape[2]
    first_block = jnp.where(own_expert == 0, 0, zero_blocks)
    last_block = jnp.where(own_expert == 0, zero_blocks, block_total)
    carried = tokens
    stored = jnp.zeros_like(tokens)
    for tick in range(segment_count):
        normed = normalize(carried, row_gain)
        gathered = lax.all_gather(normed, "shard", axis=1, tiled=True)
        partial_sum = jnp.zeros(gathered.shape, jnp.float32)

        def add_block(block_id, acc):
            block_rows = lax.dynamic_index_in_dim(gathered, block_id, 0, keepdims=False)
            result = expert_rows(block_rows, gate_part, up_part, down_part)
            return lax.dynamic_update_index_in_dim(acc, result, block_id, 0)

        partial_sum = lax.fori_loop(first_block, last_block, add_block, partial_sum)
        split_terms = partial_sum.reshape(block_total, shard_count, local_rows, width)
        received = lax.all_to_all(split_terms, "shard", split_axis=1, concat_axis=1, tiled=True)
        mixed = jnp.sum(received, axis=1)
        updated = (carried.astype(jnp.float32) + probs[:, :, None] * mixed).astype(jnp.bfloat16)
        stored = jnp.where(segment_index == tick, updated, stored)
        if tick + 1 < segment_count:
            carried = shifted(updated, "segment", 1)
    return stored[None]


def solution(mesh):
    placed = (
        P(None, "shard", None),
        P("segment", None),
        P("segment", None, "shard"),
        P("segment", None, "shard"),
        P("segment", "shard", None),
        P("segment"),
        P("segment", None, "shard"),
    )
    return jax.shard_map(
        shards,
        mesh=mesh,
        in_specs=placed,
        out_specs=P("segment", None, "shard", None),
        check_vma=False,
    )
```

profile of v0, /device:TPU:5, one launch (start us, length us, event | category | flops | bytes accessed | tf_op | source)
XLA Modules:
  0.0 946.9 jit_solution(11908347532508689451)
XLA Ops:
  9.6 82.2 %all-gather.5.cloned.1.call-done = bf16[3,128,3072]{2,0,1:T(4,128)(2,1)} async-done(((bf16[3,2,3072]{2,0,1:T(4,128)(2,1)}), bf16[3,128,3072]{2,0,1:T(4,128)(2,1)}) %all-gather.5.cloned.1.call-update) | async-done | bytes 2359312 | tf_op jit(solution)/shard_map/all_gather | solution.py:49
  91.9 4.2 copy.27
  96.1 2.7 broadcast.59.clone
  98.9 7.1 while.40
  98.9 1.7 fusion.138
  100.6 5.4 fusion.139
  106.0 6.6 reshape.46
  112.6 6.1 copy.28
  118.6 13.8 %all-to-all-start = ((f32[3,64,2,3072]{3,2,0,1:T(2,128)}), f32[3,64,2,3072]{3,2,0,1:T(2,128)}, u32[]{:S(2)}, u32[]{:S(2)}) async-start(f32[3,64,2,3072]{3,2,0,1:T(2,128)} %copy.28), calls=%async_computation | async-start | bytes 9437184 | tf_op jit(solution)/shard_map/all_to_all | solution.py:59
  132.6 107.0 %all-to-all-done = f32[3,64,2,3072]{3,2,0,1:T(2,128)} async-done(((f32[3,64,2,3072]{3,2,0,1:T(2,128)}), f32[3,64,2,3072]{3,2,0,1:T(2,128)}, u32[]{:S(2)}, u32[]{:S(2)}) %all-to-all-start) | async-done | bytes 4718624 | tf_op jit(solution)/shard_map/all_to_all | solution.py:59
  239.6 3.7 reduce_sum.73
  243.3 2.8 collective-permute-start
  246.2 1.9 collective-permute-done
  249.0 76.5 %all-gather.7.cloned.1.call-done = bf16[3,128,3072]{2,0,1:T(4,128)(2,1)} async-done(((bf16[3,2,3072]{2,0,1:T(4,128)(2,1)}), bf16[3,128,3072]{2,0,1:T(4,128)(2,1)}) %all-gather.7.cloned.1.call-update) | async-done | bytes 2359312 | tf_op jit(solution)/shard_map/all_gather | solution.py:49
  325.5 4.2 copy.30
  329.7 2.7 broadcast.59.clone.1
  332.4 7.1 while.41
  332.4 1.7 fusion.145
  334.2 5.4 fusion.146
  339.5 6.6 reshape.47
  346.1 4.0 copy.31
  350.1 120.6 %all_to_all.20 = f32[3,64,2,3072]{3,2,0,1:T(2,128)} all-to-all(f32[3,64,2,3072]{3,2,0,1:T(2,128)S(1)} %copy.31), channel_id=1, replica_groups=mesh['segment'=4,'shard'=64] {'shard'}, dimensions={1} | all-to-all | bytes 9437184 | tf_op jit(solution)/shard_map/all_to_all | solution.py:59
  470.6 3.7 reduce_sum.75
  474.4 2.8 collective-permute-start.1
  477.2 1.9 collective-permute-done.1
  480.1 76.9 %all-gather.9.cloned.1.call-done = bf16[3,128,3072]{2,0,1:T(4,128)(2,1)} async-done(((bf16[3,2,3072]{2,0,1:T(4,128)(2,1)}), bf16[3,128,3072]{2,0,1:T(4,128)(2,1)}) %all-gather.9.cloned.1.call-update) | async-done | bytes 2359312 | tf_op jit(solution)/shard_map/all_gather | solution.py:49
  557.0 4.2 copy.33
  561.2 2.7 broadcast.59.clone.2
  563.9 7.1 while.42
  563.9 1.7 fusion.152
  565.6 5.4 fusion.153
  571.0 6.6 reshape.48
  577.6 4.0 copy.34
  581.6 120.6 %all_to_all.21 = f32[3,64,2,3072]{3,2,0,1:T(2,128)} all-to-all(f32[3,64,2,3072]{3,2,0,1:T(2,128)S(1)} %copy.34), channel_id=1, replica_groups=mesh['segment'=4,'shard'=64] {'shard'}, dimensions={1} | all-to-all | bytes 9437184 | tf_op jit(solution)/shard_map/all_to_all | solution.py:59
  702.1 3.7 reduce_sum.77
  705.9 2.8 collective-permute-start.2
  708.7 1.9 collective-permute-done.2
  711.5 77.0 %all-gather.11.cloned.1.call-done = bf16[3,128,3072]{2,0,1:T(4,128)(2,1)} async-done(((bf16[3,2,3072]{2,0,1:T(4,128)(2,1)}), bf16[3,128,3072]{2,0,1:T(4,128)(2,1)}) %all-gather.11.cloned.1.call-update) | async-done | bytes 2359312 | tf_op jit(solution)/shard_map/all_gather | solution.py:49
  788.5 4.2 copy.36
  792.7 2.7 broadcast.59
  795.4 7.1 while.43
  795.4 1.7 fusion.159
  797.2 5.4 fusion.160
  802.5 6.6 reshape.49
  809.1 6.1 copy.37
  815.2 13.7 %all-to-all-start.3 = ((f32[3,64,2,3072]{3,2,0,1:T(2,128)}), f32[3,64,2,3072]{3,2,0,1:T(2,128)}, u32[]{:S(2)}, u32[]{:S(2)}) async-start(f32[3,64,2,3072]{3,2,0,1:T(2,128)} %copy.37), calls=%async_computation.3 | async-start | bytes 9437184 | tf_op jit(solution)/shard_map/all_to_all | solution.py:59
  828.9 107.1 %all-to-all-done.3 = f32[3,64,2,3072]{3,2,0,1:T(2,128)} async-done(((f32[3,64,2,3072]{3,2,0,1:T(2,128)}), f32[3,64,2,3072]{3,2,0,1:T(2,128)}, u32[]{:S(2)}, u32[]{:S(2)}) %all-to-all-start.3) | async-done | bytes 4718624 | tf_op jit(solution)/shard_map/all_to_all | solution.py:59
  936.0 3.7 reduce_sum.79
  (41 shorter events, 6.5 us)
Async XLA Ops:
  6.5 85.3 %all-gather.5.cloned.1.call-start = ((), (), s32[]{:S(2)}) async-start(), calls=%async_computation.4 | async-start | bytes 3194880 | tf_op jit(solution)/shard_map/all_gather | solution.py:49
  96.1 2.8 copy-start
  118.6 13.9 %copy-start.5 = (f32[1,3,2]{1,2,0:T(2,128)S(1)}, f32[1,3,2]{1,2,0:T(2,128)}, u32[]{:S(2)}) copy-start(f32[1,3,2]{1,2,0:T(2,128)} %param.21) | copy-start | bytes 76
  118.6 120.9 %all-to-all-start = ((f32[3,64,2,3072]{3,2,0,1:T(2,128)}), f32[3,64,2,3072]{3,2,0,1:T(2,128)}, u32[]{:S(2)}, u32[]{:S(2)}) async-start(f32[3,64,2,3072]{3,2,0,1:T(2,128)} %copy.28), calls=%async_computation | async-start | bytes 9437184 | tf_op jit(solution)/shard_map/all_to_all | solution.py:59
  132.4 110.8 %copy-start.1 = (bf16[3,2,3072]{2,1,0:T(2,128)(2,1)S(1)}, bf16[3,2,3072]{2,1,0:T(2,128)(2,1)}, u32[]{:S(2)}) copy-start(bf16[3,2,3072]{2,1,0:T(2,128)(2,1)} %param.15) | copy-start | bytes 110596
  132.4 115.8 %copy-start.2 = (f32[1,3072]{1,0:T(1,128)S(1)}, f32[1,3072]{1,0:T(1,128)}, u32[]{:S(2)}) copy-start(f32[1,3072]{1,0:T(1,128)} %param.16) | copy-start | bytes 36868
  132.4 193.1 %all-gather.7.cloned.1.call-start = ((), (), s32[]{:S(2)}) async-start(), calls=%async_computation.5 | async-start | bytes 3194880 | tf_op jit(solution)/shard_map/all_gather | solution.py:49
  243.3 4.7 collective-permute-start
  249.0 308.0 %all-gather.9.cloned.1.call-start = ((), (), s32[]{:S(2)}) async-start(), calls=%async_computation.6 | async-start | bytes 3194880 | tf_op jit(solution)/shard_map/all_gather | solution.py:49
  474.4 4.7 collective-permute-start.1
  480.0 308.5 %all-gather.11.cloned.1.call-start = ((), (), s32[]{:S(2)}) async-start(), calls=%async_computation.7 | async-start | bytes 3194880 | tf_op jit(solution)/shard_map/all_gather | solution.py:49
  705.9 89.5 %copy-start.3 = (bf16[3,2,3072]{2,1,0:T(2,128)(2,1)}, bf16[3,2,3072]{2,1,0:T(2,128)(2,1)S(1)}, u32[]{:S(2)}) copy-start(bf16[3,2,3072]{2,1,0:T(2,128)(2,1)S(1)} %fusion.87) | copy-start | bytes 110596
  705.9 4.7 collective-permute-start.2
  815.2 120.8 %all-to-all-start.3 = ((f32[3,64,2,3072]{3,2,0,1:T(2,128)}), f32[3,64,2,3072]{3,2,0,1:T(2,128)}, u32[]{:S(2)}, u32[]{:S(2)}) async-start(f32[3,64,2,3072]{3,2,0,1:T(2,128)} %copy.37), calls=%async_computation.3 | async-start | bytes 9437184 | tf_op jit(solution)/shard_map/all_to_all | solution.py:59
  828.8 110.8 %copy-start.4 = (bf16[3,2,3072]{2,1,0:T(2,128)(2,1)S(1)}, bf16[3,2,3072]{2,1,0:T(2,128)(2,1)}, u32[]{:S(2)}) copy-start(bf16[3,2,3072]{2,1,0:T(2,128)(2,1)} %copy-done.3) | copy-start | bytes 110596
Sparse Core Ops, SparseCore 0:
  10.1 81.7 all-gather.4
  249.1 76.3 all-gather.6
  480.1 76.8 all-gather.8
  711.6 76.8 all-gather.10
where the time goes:
time: 949 us; the launch traced here: 947 us
  waiting for transfers between devices  532 us (56%)
  blocking collectives  241 us (25%)
  local copies, waits for them, and re-layouts  76.8 us (8%)
  starting transfers between devices  36 us (4%)
  matrix products  28.3 us (3%)
  other arithmetic  18.2 us (2%)
  between operations  14 us (1%)
    all_gather x4, waiting for transfers between devices, shards(): gathered = lax.all_gather(normed, 'shard', axis=1, tiled=True)  313 us
    all_to_all x2, blocking collectives, shards(): lax.all_to_all(split_terms, 'shard', split_axis=1, concat_axis=1, tiled=T...  241 us
    all_to_all x2, waiting for transfers between devices, shards(): lax.all_to_all(split_terms, 'shard', split_axis=1, concat_axis=1, tiled=T...  214 us
    reshape x8, local copies, waits for them, and re-layouts, shards(): partial_sum.reshape(block_total, shard_count, local_rows, width)  46.4 us
    all_to_all x2, starting transfers between devices, shards(): lax.all_to_all(split_terms, 'shard', split_axis=1, concat_axis=1, tiled=T...  27.4 us
    dot_general x4, matrix products, expert_rows(): return jnp.dot(hidden, down_part, preferred_element_type=jnp.float32)  21.5 us
  transfers between devices with their start and end apart: 9, of which 9 were waited for; matrix products, arithmetic and copies ran while one was open for 0% of the time, Pallas kernels for 0%

commit v1 on v0

--- a/solution.py
+++ b/solution.py
@@ -1,9 +1,23 @@
+import functools
 import jax
 import jax.numpy as jnp
 from jax import lax
 from jax.sharding import PartitionSpec as P
 
 FF = 16384
+
+
+def handle_stocks(body, dev_axis):
+    mat_out = jnp.concatenate(
+        jax.lax.all_to_all(
+            jnp.stack([body for _ in range(jax.lax.axis_size(dev_axis))]), dev_axis, 0, 0
+        ),
+        axis=1,
+    )
+    return mat_out
+
+
+paths_pass = functools.partial(handle_stocks, dev_axis="shard")
 
 
 def shifted(value, axis, steps):
@@ -46,7 +60,7 @@
     stored = jnp.zeros_like(tokens)
     for tick in range(segment_count):
         normed = normalize(carried, row_gain)
-        gathered = lax.all_gather(normed, "shard", axis=1, tiled=True)
+        gathered = paths_pass(normed)
         partial_sum = jnp.zeros(gathered.shape, jnp.float32)
 
         def add_block(block_id, acc):

time: 949 us -> 920 us (0.969)
  waiting for transfers between devices: 532 us -> 389 us
  blocking collectives: 241 us -> 305 us
  local copies, waits for them, and re-layouts: 76.8 us -> 106 us
  starting transfers between devices: 36 us -> 62.5 us
  between operations: 14 us -> 1.09 us
    all_gather x4 -> x0, waiting for transfers between devices: 313 us -> none  [shards(): gathered = lax.all_gather(normed, 'shard', axis=1, tiled=True)]
    all_to_all x0 -> x3, waiting for transfers between devices: none -> 169 us  [handle_stocks(): jax.lax.all_to_all(jnp.stack([body for _ in range(jax.lax.axis_size(dev_a...]
    all_to_all x0 -> x1, blocking collectives: none -> 64.2 us  [handle_stocks(): jax.lax.all_to_all(jnp.stack([body for _ in range(jax.lax.axis_size(dev_a...]
    reshape x0 -> x8, local copies, waits for them, and re-layouts: none -> 39.5 us  [handle_stocks(): jnp.concatenate(jax.lax.all_to_all(jnp.stack([body for _ in range(jax.lax...]
    all_to_all x0 -> x3, starting transfers between devices: none -> 27.1 us  [handle_stocks(): jax.lax.all_to_all(jnp.stack([body for _ in range(jax.lax.axis_size(dev_a...]
    while x4 -> x0, local copies, waits for them, and re-layouts: 16.9 us -> none  [shards(): partial_sum = lax.fori_loop(first_block, last_block, add_block, partial_sum)]
    another operation x4 -> x8, local copies, waits for them, and re-layouts: 10.8 us -> 19.8 us
  transfers between devices with their start and end apart: 9 -> 8, of which waited for: 9 -> 8; matrix products, arithmetic and copies ran while one was open for 0% -> 0% of each run, Pallas kernels for 0% -> 0%
where the time goes in v1:
time: 920 us; the launch traced here: 910 us
  waiting for transfers between devices  389 us (42%)
  blocking collectives  305 us (33%)
  local copies, waits for them, and re-layouts  106 us (12%)
  starting transfers between devices  62.5 us (7%)
  matrix products  28.3 us (3%)
  other arithmetic  18.2 us (2%)
    all_to_all x2, blocking collectives, shards(): lax.all_to_all(split_terms, 'shard', split_axis=1, concat_axis=1, tiled=T...  241 us
    all_to_all x2, waiting for transfers between devices, shards(): lax.all_to_all(split_terms, 'shard', split_axis=1, concat_axis=1, tiled=T...  214 us
    all_to_all x3, waiting for transfers between devices, handle_stocks(): jax.lax.all_to_all(jnp.stack([body for _ in range(jax.lax.axis_size(dev_a...  169 us
    all_to_all x1, blocking collectives, handle_stocks(): jax.lax.all_to_all(jnp.stack([body for _ in range(jax.lax.axis_size(dev_a...  64.2 us
    reshape x8, local copies, waits for them, and re-layouts, shards(): partial_sum.reshape(block_total, shard_count, local_rows, width)  46.5 us
    reshape x8, local copies, waits for them, and re-layouts, handle_stocks(): jnp.concatenate(jax.lax.all_to_all(jnp.stack([body for _ in range(jax.lax...  39.5 us
    all_to_all x3, starting transfers between devices, handle_stocks(): jax.lax.all_to_all(jnp.stack([body for _ in range(jax.lax.axis_size(dev_a...  27.1 us
    all_to_all x2, starting transfers between devices, shards(): lax.all_to_all(split_terms, 'shard', split_axis=1, concat_axis=1, tiled=T...  26.9 us
  transfers between devices with their start and end apart: 8, of which 8 were waited for; matrix products, arithmetic and copies ran while one was open for 0% of the time, Pallas kernels for 0%

profile of v1, /device:TPU:5, one launch (start us, length us, event | category | flops | bytes accessed | tf_op | source)
XLA Modules:
  0.0 909.9 jit_solution(18052100580221268120)
XLA Ops:
  4.4 12.3 %all-to-all-start = ((bf16[64,3,2,3072]{3,2,1,0:T(2,128)(2,1)}), bf16[64,3,2,3072]{3,2,1,0:T(2,128)(2,1)S(1)}, u32[]{:S(2)}, u32[]{:S(2)}) async-start(bf16[64,3,2,3072]{3,2,1,0:T(2,128)(2,1)} %stack.8), calls=%async_computation | async-start | bytes 4718592 | tf_op jit(solution)/shard_map/all_to_all | solution.py:12
  17.4 56.0 %all-to-all-done = bf16[64,3,2,3072]{3,2,1,0:T(2,128)(2,1)S(1)} async-done(((bf16[64,3,2,3072]{3,2,1,0:T(2,128)(2,1)}), bf16[64,3,2,3072]{3,2,1,0:T(2,128)(2,1)S(1)}, u32[]{:S(2)}, u32[]{:S(2)}) %all-to-all-start) | async-done | bytes 2359328 | tf_op jit(solution)/shard_map/all_to_all | solution.py:12
  73.4 3.0 copy.11
  76.4 6.0 reshape.79
  82.4 2.7 broadcast.67.clone
  85.2 7.1 while.40
  87.0 5.4 fusion.139
  92.3 6.6 reshape.80
  98.9 6.1 copy.12
  105.0 13.7 %all-to-all-start.1 = ((f32[3,64,2,3072]{3,2,0,1:T(2,128)}), f32[3,64,2,3072]{3,2,0,1:T(2,128)}, u32[]{:S(2)}, u32[]{:S(2)}) async-start(f32[3,64,2,3072]{3,2,0,1:T(2,128)} %copy.12), calls=%async_computation.1 | async-start | bytes 9437184 | tf_op jit(solution)/shard_map/all_to_all | solution.py:73
  118.8 106.8 %all-to-all-done.1 = f32[3,64,2,3072]{3,2,0,1:T(2,128)} async-done(((f32[3,64,2,3072]{3,2,0,1:T(2,128)}), f32[3,64,2,3072]{3,2,0,1:T(2,128)}, u32[]{:S(2)}, u32[]{:S(2)}) %all-to-all-start.1) | async-done | bytes 4718624 | tf_op jit(solution)/shard_map/all_to_all | solution.py:73
  225.7 3.7 reduce_sum.73
  229.4 2.8 collective-permute-start
  237.0 7.2 all-to-all-start.2
  244.2 56.6 %all-to-all-done.2 = bf16[64,3,2,3072]{3,2,1,0:T(2,128)(2,1)} async-done(((bf16[64,3,2,3072]{3,2,1,0:T(2,128)(2,1)}), bf16[64,3,2,3072]{3,2,1,0:T(2,128)(2,1)}, u32[]{:S(2)}, u32[]{:S(2)}) %all-to-all-start.2) | async-done | bytes 2359328 | tf_op jit(solution)/shard_map/all_to_all | solution.py:12
  300.8 4.7 copy.13
  305.4 6.0 reshape.82
  311.5 2.7 broadcast.67.clone.1
  314.1 7.1 while.41
  315.9 5.4 fusion.146
  321.2 6.6 reshape.83
  327.8 4.0 copy.14
  331.8 120.2 %all_to_all.41 = f32[3,64,2,3072]{3,2,0,1:T(2,128)} all-to-all(f32[3,64,2,3072]{3,2,0,1:T(2,128)S(1)} %copy.14), channel_id=1, replica_groups=mesh['segment'=4,'shard'=64] {'shard'}, dimensions={1} | all-to-all | bytes 9437184 | tf_op jit(solution)/shard_map/all_to_all | solution.py:73
  451.9 3.7 reduce_sum.75
  455.7 2.8 collective-permute-start.1
  463.3 7.6 all-to-all-start.4
  470.9 56.6 %all-to-all-done.4 = bf16[64,3,2,3072]{3,2,1,0:T(2,128)(2,1)} async-done(((bf16[64,3,2,3072]{3,2,1,0:T(2,128)(2,1)}), bf16[64,3,2,3072]{3,2,1,0:T(2,128)(2,1)}, u32[]{:S(2)}, u32[]{:S(2)}) %all-to-all-start.4) | async-done | bytes 2359328 | tf_op jit(solution)/shard_map/all_to_all | solution.py:12
  527.5 4.7 copy.15
  532.1 6.0 reshape.85
  538.2 2.7 broadcast.67.clone.2
  540.9 7.1 while.42
  542.6 5.4 fusion.153
  547.9 6.6 reshape.86
  554.5 4.0 copy.16
  558.5 120.6 %all_to_all.42 = f32[3,64,2,3072]{3,2,0,1:T(2,128)} all-to-all(f32[3,64,2,3072]{3,2,0,1:T(2,128)S(1)} %copy.16), channel_id=1, replica_groups=mesh['segment'=4,'shard'=64] {'shard'}, dimensions={1} | all-to-all | bytes 9437184 | tf_op jit(solution)/shard_map/all_to_all | solution.py:73
  679.1 3.7 reduce_sum.77
  682.8 2.8 collective-permute-start.2
  689.0 64.2 %all_to_all.40 = bf16[64,3,2,3072]{3,2,1,0:T(2,128)(2,1)S(1)} all-to-all(bf16[64,3,2,3072]{3,2,1,0:T(2,128)(2,1)S(1)} %stack.11), channel_id=1, replica_groups=mesh['segment'=4,'shard'=64] {'shard'}, dimensions={0} | all-to-all | bytes 4718592 | tf_op jit(solution)/shard_map/all_to_all | solution.py:12
  753.2 3.0 copy.17
  756.2 6.0 reshape.88
  762.2 2.7 broadcast.67
  764.9 7.2 while.43
  766.7 5.4 fusion.160
  772.2 6.6 reshape.89
  778.8 6.1 copy.18
  784.9 13.3 %all-to-all-start.7 = ((f32[3,64,2,3072]{3,2,0,1:T(2,128)}), f32[3,64,2,3072]{3,2,0,1:T(2,128)}, u32[]{:S(2)}, u32[]{:S(2)}) async-start(f32[3,64,2,3072]{3,2,0,1:T(2,128)} %copy.18), calls=%async_computation.7 | async-start | bytes 9437184 | tf_op jit(solution)/shard_map/all_to_all | solution.py:73
  798.2 107.1 %all-to-all-done.7 = f32[3,64,2,3072]{3,2,0,1:T(2,128)} async-done(((f32[3,64,2,3072]{3,2,0,1:T(2,128)}), f32[3,64,2,3072]{3,2,0,1:T(2,128)}, u32[]{:S(2)}, u32[]{:S(2)}) %all-to-all-start.7) | async-done | bytes 4718624 | tf_op jit(solution)/shard_map/all_to_all | solution.py:73
  905.3 3.7 reduce_sum.79
  (40 shorter events, 25.3 us)
Async XLA Ops:
  4.4 69.0 %all-to-all-start = ((bf16[64,3,2,3072]{3,2,1,0:T(2,128)(2,1)}), bf16[64,3,2,3072]{3,2,1,0:T(2,128)(2,1)S(1)}, u32[]{:S(2)}, u32[]{:S(2)}) async-start(bf16[64,3,2,3072]{3,2,1,0:T(2,128)(2,1)} %stack.8), calls=%async_computation | async-start | bytes 4718592 | tf_op jit(solution)/shard_map/all_to_all | solution.py:12
  82.4 2.8 copy-start
  105.0 13.7 %copy-start.5 = (f32[1,3,2]{1,2,0:T(2,128)S(1)}, f32[1,3,2]{1,2,0:T(2,128)}, u32[]{:S(2)}) copy-start(f32[1,3,2]{1,2,0:T(2,128)} %param.21) | copy-start | bytes 76
  105.0 120.7 %all-to-all-start.1 = ((f32[3,64,2,3072]{3,2,0,1:T(2,128)}), f32[3,64,2,3072]{3,2,0,1:T(2,128)}, u32[]{:S(2)}, u32[]{:S(2)}) async-start(f32[3,64,2,3072]{3,2,0,1:T(2,128)} %copy.12), calls=%async_computation.1 | async-start | bytes 9437184 | tf_op jit(solution)/shard_map/all_to_all | solution.py:73
  118.7 110.6 %copy-start.1 = (bf16[3,2,3072]{2,1,0:T(2,128)(2,1)S(1)}, bf16[3,2,3072]{2,1,0:T(2,128)(2,1)}, u32[]{:S(2)}) copy-start(bf16[3,2,3072]{2,1,0:T(2,128)(2,1)} %param.15) | copy-start | bytes 110596
  118.7 115.6 %copy-start.2 = (f32[1,3072]{1,0:T(1,128)S(1)}, f32[1,3072]{1,0:T(1,128)}, u32[]{:S(2)}) copy-start(f32[1,3072]{1,0:T(1,128)} %param.16) | copy-start | bytes 36868
  229.4 4.7 collective-permute-start
  237.0 63.8 %all-to-all-start.2 = ((bf16[64,3,2,3072]{3,2,1,0:T(2,128)(2,1)}), bf16[64,3,2,3072]{3,2,1,0:T(2,128)(2,1)}, u32[]{:S(2)}, u32[]{:S(2)}) async-start(bf16[64,3,2,3072]{3,2,1,0:T(2,128)(2,1)} %stack.9), calls=%async_computation.2 | async-start | bytes 4718592 | tf_op jit(solution)/shard_map/all_to_all | solution.py:12
  455.7 4.7 collective-permute-start.1
  463.3 64.2 %all-to-all-start.4 = ((bf16[64,3,2,3072]{3,2,1,0:T(2,128)(2,1)}), bf16[64,3,2,3072]{3,2,1,0:T(2,128)(2,1)}, u32[]{:S(2)}, u32[]{:S(2)}) async-start(bf16[64,3,2,3072]{3,2,1,0:T(2,128)(2,1)} %stack.10), calls=%async_computation.4 | async-start | bytes 4718592 | tf_op jit(solution)/shard_map/all_to_all | solution.py:12
  682.8 70.4 %copy-start.3 = (bf16[3,2,3072]{2,1,0:T(2,128)(2,1)}, bf16[3,2,3072]{2,1,0:T(2,128)(2,1)S(1)}, u32[]{:S(2)}) copy-start(bf16[3,2,3072]{2,1,0:T(2,128)(2,1)S(1)} %fusion.87) | copy-start | bytes 110596
  682.8 4.7 collective-permute-start.2
  784.9 120.4 %all-to-all-start.7 = ((f32[3,64,2,3072]{3,2,0,1:T(2,128)}), f32[3,64,2,3072]{3,2,0,1:T(2,128)}, u32[]{:S(2)}, u32[]{:S(2)}) async-start(f32[3,64,2,3072]{3,2,0,1:T(2,128)} %copy.18), calls=%async_computation.7 | async-start | bytes 9437184 | tf_op jit(solution)/shard_map/all_to_all | solution.py:73
  798.1 110.8 %copy-start.4 = (bf16[3,2,3072]{2,1,0:T(2,128)(2,1)S(1)}, bf16[3,2,3072]{2,1,0:T(2,128)(2,1)}, u32[]{:S(2)}) copy-start(bf16[3,2,3072]{2,1,0:T(2,128)(2,1)} %copy-done.3) | copy-start | bytes 110596
